TPU v7x, 32 devices: a whole 2x2x4 slice. The times are simulated.
32 devices in a mesh: row: 4 (over x, core), col: 8 (over z, y).
Axes of the slice: x: 2, y: 2, z: 4, core: 2. Of those that a mesh axis runs over, the one named last changes fastest.
Arguments:
- pair: bfloat16 [768, 768, 512], P('row', 'col'), may hold values from -6 to 6
- w_bias: bfloat16 [512, 96], replicated, may hold values from -0.25 to 0.25
- queries: bfloat16 [768, 1536], P('row', 'col'), may hold values from -360 to 360
- keys: bfloat16 [768, 1536], P('col', 'row'), may hold values from -6 to 6
- values: bfloat16 [768, 1536], P('col', 'row'), may hold values from -6 to 6
- d_out: bfloat16 [768, 1536], P('row', 'col'), may hold values from -6 to 6
Outputs:
- d_pair: bfloat16 [768, 768, 512], P('row', 'col')
- d_wbias: float32 [512, 96], replicated
- d_queries: bfloat16 [768, 1536], P('row', 'col')
- d_keys: bfloat16 [768, 1536], P('col', 'row')
- d_values: bfloat16 [768, 1536], P('col', 'row')
All inputs are finite; a program needn't handle non-finite values.
Results may differ from a plain program's by a relative error of at most 0.0095.
Values may be sent and summed in bfloat16 or wider, within the bound.
A program may use at most 128 MiB of HBM per device.

v0:
```python
import jax
import jax.numpy as jnp
from jax import lax
from jax.sharding import PartitionSpec as P

D = 1536
H = 96
P_SIZE = 512
HD = 16


def joined(value, axis, join):
    pieces = jax.tree.map(lambda part: lax.all_gather(part, axis), value)
    head = jax.tree.map(lambda part: part[0], pieces)
    tail = jax.tree.map(lambda part: part[1:], pieces)
    subtotal, _ = lax.scan(lambda subtotal, piece: (join(subtotal, piece), None), head, tail)
    return subtotal


def combine_stats(former, latter):
    joined_max = jnp.maximum(former[0], latter[0])
    scale_former = jnp.exp(former[0] - joined_max)
    scale_latter = jnp.exp(latter[0] - joined_max)
    return (
        joined_max,
        former[1] * scale_former + latter[1] * scale_latter,
        former[2] * scale_former + latter[2] * scale_latter,
    )


def on_device(pair, w_bias, queries, keys, values, d_out):
    row_count = pair.shape[0]
    col_count = pair.shape[1]
    query_full, out_full = (
        lax.all_gather(queries, "col", axis=1, tiled=True),
        lax.all_gather(d_out, "col", axis=1, tiled=True),
    )
    key_full, value_full = (
        lax.all_gather(keys, "row", axis=1, tiled=True),
        lax.all_gather(values, "row", axis=1, tiled=True),
    )
    query_heads = query_full.reshape(row_count, H, HD)
    out_heads = out_full.reshape(row_count, H, HD)
    key_heads = key_full.reshape(col_count, H, HD)
    value_heads = value_full.reshape(col_count, H, HD)
    flat_pair = pair.reshape(row_count * col_count, P_SIZE)
    pair_bias = jnp.dot(flat_pair, w_bias, preferred_element_type=jnp.float32).reshape(
        row_count, col_count, H
    )
    scale = 1.0 / HD**0.5
    scores = jnp.einsum(
        "ihd,jhd->hij", query_heads, key_heads, preferred_element_type=jnp.float32
    ) * scale + pair_bias.transpose(2, 0, 1)
    grad_prob = jnp.einsum(
        "ihd,jhd->hij", out_heads, value_heads, preferred_element_type=jnp.float32
    )
    local_max = jnp.max(scores, axis=-1)
    exp_scores = jnp.exp(scores - local_max[..., None])
    local_stats = (
        local_max,
        jnp.sum(exp_scores, axis=-1),
        jnp.sum(exp_scores * grad_prob, axis=-1),
    )
    row_max, row_total, row_upper = joined(local_stats, "col", combine_stats)
    weights = jnp.exp(scores - row_max[..., None]) / row_total[..., None]
    row_delta = row_upper / row_total
    grad_score = (weights * (grad_prob - row_delta[..., None])).astype(jnp.bfloat16)
    weights_low = weights.astype(jnp.bfloat16)
    score_flat = grad_score.transpose(1, 2, 0).reshape(row_count * col_count, H)
    d_pair = (
        jnp.dot(score_flat, w_bias.T, preferred_element_type=jnp.float32)
        .astype(jnp.bfloat16)
        .reshape(row_count, col_count, P_SIZE)
    )
    weight_term = jnp.dot(flat_pair.T, score_flat, preferred_element_type=jnp.float32)
    d_wbias = lax.psum(weight_term, ("row", "col"))
    query_term = (
        jnp.einsum("hij,jhd->ihd", grad_score, key_heads, preferred_element_type=jnp.float32)
        * scale
    ).reshape(row_count, D)
    key_term = (
        jnp.einsum("hij,ihd->jhd", grad_score, query_heads, preferred_element_type=jnp.float32)
        * scale
    ).reshape(col_count, D)
    value_term = jnp.einsum(
        "hij,ihd->jhd", weights_low, out_heads, preferred_element_type=jnp.float32
    ).reshape(col_count, D)
    query_grad = lax.psum_scatter(query_term, "col", scatter_dimension=1, tiled=True)
    key_grad, value_grad = (
        lax.psum_scatter(key_term, "row", scatter_dimension=1, tiled=True),
        lax.psum_scatter(value_term, "row", scatter_dimension=1, tiled=True),
    )
    return (
        d_pair,
        d_wbias,
        query_grad.astype(jnp.bfloat16),
        key_grad.astype(jnp.bfloat16),
        value_grad.astype(jnp.bfloat16),
    )


def solution(mesh):
    return jax.shard_map(
        on_device,
        mesh=mesh,
        in_specs=(
            P("row", "col", None),
            P(),
            P("row", "col"),
            P("col", "row"),
            P("col", "row"),
            P("row", "col"),
        ),
        out_specs=(P("row", "col", None), P(), P("row", "col"), P("col", "row"), P("col", "row")),
        check_vma=False,
    )
```

profile of v0, /device:TPU:8, one launch (start us, length us, event | category | flops | bytes accessed | tf_op | source)
XLA Modules:
  0.0 433.7 jit_solution(17199849973470065205)
XLA Ops:
  8.9 11.2 %fusion.11 = f32[192,96,96]{2,1,0:T(8,128)} fusion(bf16[192,96,512]{2,1,0:T(8,128)(2,1)} %param.8, bf16[512,96]{0,1:T(8,128)(2,1)S(1)} %copy-done), kind=kOutput, calls=%fused_computation.27 | convolution fusion | flops 1811939328 | bytes 26050560 | tf_op jit(solution)/shard_map/dot_general | solution.py:47
  20.1 12.1 %copy.40 = f32[192,96,96]{0,1,2:T(8,128)} copy(f32[192,96,96]{2,1,0:T(8,128)} %fusion.11) | data formatting | bytes 14155776 | tf_op jit(solution)/shard_map/dot_general | solution.py:47
  32.4 29.7 %all_gather.30 = bf16[192,1536]{0,1:T(8,128)(2,1)S(1)} all-gather(bf16[192,192]{0,1:T(8,128)(2,1)S(1)} %copy.38), channel_id=1, replica_groups=mesh['row'=4,'col'=8] {'col'}, dimensions={1}, use_global_device_ids=true | all-gather | bytes 663552 | tf_op jit(solution)/shard_map/all_gather | solution.py:35
  62.1 5.9 %all_gather.31 = bf16[96,1536]{1,0:T(8,128)(2,1)S(1)} all-gather(bf16[96,384]{1,0:T(8,128)(2,1)S(1)} %copy-done.5), channel_id=1, replica_groups=mesh['row'=4,'col'=8] {'row'}, dimensions={1}, use_global_device_ids=true | all-gather | bytes 368640 | tf_op jit(solution)/shard_map/all_gather | solution.py:39
  68.4 32.2 %all_gather.36 = bf16[192,1536]{0,1:T(8,128)(2,1)S(1)} all-gather(bf16[192,192]{0,1:T(8,128)(2,1)S(1)} %copy.42), channel_id=1, replica_groups=mesh['row'=4,'col'=8] {'col'}, dimensions={1}, use_global_device_ids=true | all-gather | bytes 663552 | tf_op jit(solution)/shard_map/all_gather | solution.py:36
  100.6 5.9 %all_gather.37 = bf16[96,1536]{1,0:T(8,128)(2,1)S(1)} all-gather(bf16[96,384]{1,0:T(8,128)(2,1)S(1)} %copy-done.6), channel_id=1, replica_groups=mesh['row'=4,'col'=8] {'row'}, dimensions={1}, use_global_device_ids=true | all-gather | bytes 368640 | tf_op jit(solution)/shard_map/all_gather | solution.py:40
  106.7 9.2 %fusion.13 = (f32[96,192]{1,0:T(8,128)S(1)}, f32[96,192,96]{1,2,0:T(8,128)S(1)}, f32[96,192,96]{1,2,0:T(8,128)}) fusion(f32[192,96,96]{0,1,2:T(8,128)} %copy.40, bf16[192,96,16]{0,2,1:T(8,128)(2,1)S(1)} %bitcast.92, bf16[96,96,16]{0,2,1:T(8,128)(2,1)S(1)} %bitcast.96), kind=kOutput, calls=%fused_computation.29 | convolution fusion | flops 61913088 | bytes 22192128 | tf_op jit(solution)/shard_map/ihd,jhd->hij/dot_general | solution.py:51
  115.8 5.7 %multiply_reduce_fusion = (f32[96,192]{1,0:T(8,128)S(1)}, f32[96,192]{1,0:T(8,128)S(1)}, f32[96,192,96]{1,2,0:T(8,128)}) fusion(f32[96,192,96]{1,2,0:T(8,128)S(1)} %get-tuple-element.66, f32[96,192]{1,0:T(8,128)S(1)} %get-tuple-element.65, bf16[192,96,16]{0,2,1:T(8,128)(2,1)S(1)} %bitcast.98, bf16[96,96,16]{0,2,1:T(8,128)(2,1)S(1)} %bitcast.103), kind=kOutput, calls=%fused_computation.19 | convolution fusion | flops 63664128 | bytes 15261696 | tf_op jit(solution)/shard_map/ihd,jhd->hij/dot_general | solution.py:54
  122.1 32.1 %all-gather.1 = f32[768,192]{1,0:T(8,128)S(1)} all-gather(f32[96,192]{1,0:T(8,128)S(1)} %get-tuple-element.48), channel_id=3, replica_groups=mesh['row'=4,'col'=8] {'col'}, dimensions={0}, use_global_device_ids=true | all-gather | bytes 663552 | tf_op jit(solution)/shard_map/all_gather | solution.py:13
  155.2 32.1 %all-gather.2 = f32[768,192]{1,0:T(8,128)S(1)} all-gather(f32[96,192]{1,0:T(8,128)S(1)} %get-tuple-element.47), channel_id=4, replica_groups=mesh['row'=4,'col'=8] {'col'}, dimensions={0}, use_global_device_ids=true | all-gather | bytes 663552 | tf_op jit(solution)/shard_map/all_gather | solution.py:13
  188.2 32.0 %all-gather = f32[768,192]{1,0:T(8,128)S(1)} all-gather(f32[96,192]{1,0:T(8,128)S(1)} %get-tuple-element.65), channel_id=2, replica_groups=mesh['row'=4,'col'=8] {'col'}, dimensions={0}, use_global_device_ids=true | all-gather | bytes 663552 | tf_op jit(solution)/shard_map/all_gather | solution.py:13
  220.3 13.8 %while.14 = (s32[]{:T(128)}, f32[96,192]{1,0:T(8,128)S(1)}, f32[96,192]{1,0:T(8,128)S(1)}, f32[96,192]{1,0:T(8,128)S(1)}, f32[7,96,192]{2,1,0:T(8,128)S(1)}, /*i...) while((s32[]{:T(128)}, f32[96,192]{1,0:T(8,128)S(1)}, f32[96,192]{1,0:T(8,128)S(1)}, ...), condition=%wide.region_4.5_spmd, body=%wide.region_3.4_spmd.sunk | while | flops 202754 | bytes 1032285 | solution.py:16
  234.2 6.2 %fusion.9 = f32[96,96,16]{1,2,0:T(8,128)} fusion(bf16[192,96,16]{0,2,1:T(8,128)(2,1)S(1)} %bitcast.99, f32[96,192,96]{1,2,0:T(8,128)} %copy-done.1, f32[96,192]{1,0:T(8,128)S(1)} %get-tuple-element.45, f32[96,192]{1,0:T(8,128)S(1)} %get-tuple-element.44), kind=kOutput, calls=%fused_computation.22 | convolution fusion | flops 61931520 | bytes 8404992 | tf_op jit(solution)/shard_map/hij,ihd->jhd/dot_general | solution.py:85
  240.3 2.2 copy.51
  242.8 7.9 %multiply_convert_fusion = bf16[96,192,96]{1,2,0:T(8,128)(2,1)S(1)} fusion(f32[96,192,96]{1,2,0:T(8,128)} %get-tuple-element.68, f32[96,192]{1,0:T(8,128)S(1)} %div.21, f32[96,192]{1,0:T(8,128)S(1)} %get-tuple-element.45, f32[96,192,96]{1,2,0:T(8,128)} %copy-done.1, f32[96,192]{1,0:T(8,128)S(1)} %get-tuple-element.44), kind=kLoop, calls=%fused_computation.17 | loop fusion | flops 8847360 | bytes 17915904 | tf_op jit(solution)/shard_map/convert_element_type | solution.py:67
  255.4 4.2 convolution_multiply_fusion
  259.7 13.1 %fusion.4 = bf16[192,96,96]{0,1,2:T(8,128)(2,1)} fusion(f32[96,192,96]{1,2,0:T(8,128)} %get-tuple-element.68, f32[192,96,96]{0,1,2:T(8,128)} %copy.40, f32[96,192,96]{1,2,0:T(8,128)} %get-tuple-element.67, f32[192,96]{0,1:T(8,128)S(1)} %bitcast.104, f32[192,96]{0,1:T(8,128)S(1)} %bitcast.91, f32[192,96]{0,1:T(8,128)S(1)} %bitcast.90), kind=kLoop, calls=%fused_computation.11 | loop fusion | flops 12386304 | bytes 24993792 | tf_op jit(solution)/shard_map/convert_element_type | solution.py:67
  272.8 7.6 %copy.45 = bf16[192,96,96]{1,2,0:T(8,128)(2,1)} copy(bf16[192,96,96]{0,1,2:T(8,128)(2,1)} %fusion.4) | data formatting | bytes 7077888 | tf_op jit(solution)/shard_map/convert_element_type | solution.py:67
  280.5 11.8 %convolution_bitcast_fusion = f32[512,96]{0,1:T(8,128)} fusion(bf16[192,96,96]{1,2,0:T(8,128)(2,1)} %copy.45, bf16[192,96,512]{2,1,0:T(8,128)(2,1)} %param.8), kind=kOutput, calls=%fused_computation.26 | convolution fusion | flops 1811939328 | bytes 22609920 | tf_op jit(solution)/shard_map/dot_general | solution.py:75
  292.2 6.7 %copy.44 = bf16[192,96,96]{1,0,2:T(8,128)(2,1)} copy(bf16[192,96,96]{0,1,2:T(8,128)(2,1)} %fusion.4) | data formatting | bytes 7077888 | tf_op jit(solution)/shard_map/convert_element_type | solution.py:67
  299.0 9.2 %reshape.49 = bf16[18432,96]{0,1:T(8,128)(2,1)} reshape(bf16[192,96,96]{1,0,2:T(8,128)(2,1)} %copy.44) | data formatting | bytes 7077888 | tf_op jit(solution)/shard_map/reshape | solution.py:69
  308.2 11.5 %convolution_convert_fusion = bf16[18432,512]{1,0:T(8,128)(2,1)} fusion(bf16[18432,96]{0,1:T(8,128)(2,1)} %reshape.49, bf16[512,96]{0,1:T(8,128)(2,1)S(1)} %copy-done), kind=kOutput, calls=%fused_computation.8 | convolution fusion | flops 1821376512 | bytes 22511616 | tf_op jit(solution)/shard_map/dot_general | solution.py:71
  322.8 38.5 %reduce-scatter.10.cloned.1.call-done = f32[192,192]{1,0:T(8,128)} async-done(((f32[1536,192]{1,0:T(8,128)}), f32[192,192]{1,0:T(8,128)}) %reduce-scatter.10.cloned.1.call-update) | async-done | bytes 147472
  363.0 61.9 %all-reduce.2.cloned.1.call-done = f32[512,96]{0,1:T(8,128)} async-done(((f32[512,96]{0,1:T(8,128)}), f32[512,96]{0,1:T(8,128)}) %all-reduce.2.cloned.1.call-update) | async-done | bytes 196624 | tf_op jit(solution)/shard_map/psum | solution.py:76
  (62 shorter events, 29.1 us)
Async XLA Ops:
  8.0 0.9 copy-start
  8.0 311.7 %reduce-scatter.8.cloned.1.call-start = ((), (), s32[]{:S(2)}) async-start(), calls=%async_computation.5 | async-start | bytes 737280 | tf_op jit(solution)/shard_map/reduce_scatter | solution.py:91
  20.1 12.2 %copy-start.3 = (bf16[192,192]{1,0:T(8,128)(2,1)S(1)}, bf16[192,192]{1,0:T(8,128)(2,1)}, u32[]{:S(2)}) copy-start(bf16[192,192]{1,0:T(8,128)(2,1)} %param.10) | copy-start | bytes 221188
  20.1 42.0 %copy-start.5 = (bf16[96,384]{1,0:T(8,128)(2,1)S(1)}, bf16[96,384]{1,0:T(8,128)(2,1)}, u32[]{:S(2)}) copy-start(bf16[96,384]{1,0:T(8,128)(2,1)} %param.11) | copy-start | bytes 221188
  20.1 48.1 %copy-start.4 = (bf16[192,192]{1,0:T(8,128)(2,1)S(1)}, bf16[192,192]{1,0:T(8,128)(2,1)}, u32[]{:S(2)}) copy-start(bf16[192,192]{1,0:T(8,128)(2,1)} %param.13) | copy-start | bytes 221188
  20.1 80.5 %copy-start.6 = (bf16[96,384]{1,0:T(8,128)(2,1)S(1)}, bf16[96,384]{1,0:T(8,128)(2,1)}, u32[]{:S(2)}) copy-start(bf16[96,384]{1,0:T(8,128)(2,1)} %param.12) | copy-start | bytes 221188
  115.8 6.3 %copy-start.1 = (f32[96,192,96]{1,2,0:T(8,128)}, f32[96,192,96]{1,2,0:T(8,128)S(1)}, u32[]{:S(2)}) copy-start(f32[96,192,96]{1,2,0:T(8,128)S(1)} %get-tuple-element.66) | copy-start | bytes 21233668
  242.6 78.7 %reduce-scatter.6.cloned.1.call-start = ((), (), s32[]{:S(2)}) async-start(), calls=%async_computation.4 | async-start | bytes 737280 | tf_op jit(solution)/shard_map/reduce_scatter | solution.py:90
  250.7 2.2 copy-start.2
  255.4 106.0 %reduce-scatter.10.cloned.1.call-start = ((), (), s32[]{:S(2)}) async-start(), calls=%async_computation.6 | async-start | bytes 1769472
  259.7 165.3 %all-reduce.2.cloned.1.call-start = ((), (), s32[]{:S(2)}) async-start(), calls=%async_computation.3 | async-start | bytes 393216 | tf_op jit(solution)/shard_map/psum | solution.py:76
Sparse Core Ops, SparseCore 0:
  242.7 25.4 reduce-scatter.7
  270.7 22.0 reduce-scatter.5
  296.2 65.0 reduce-scatter.9
Sparse Core Ops, SparseCore 1:
  292.3 132.6 all-reduce.1
where the time goes:
time: 435 us; the launch traced here: 434 us
  blocking collectives  170 us (39%)
  waiting for transfers between devices  101 us (23%)
  matrix products  61.1 us (14%)
  local copies, waits for them, and re-layouts  48.6 us (11%)
  other arithmetic  37.7 us (9%)
  between operations  15.3 us (4%)
    all_gather x3, blocking collectives, joined(): pieces = jax.tree.map(lambda part: lax.all_gather(part, axis), value)  96.3 us
    psum x1, waiting for transfers between devices, on_device(): d_wbias = lax.psum(weight_term, ('row', 'col'))  61.9 us
    unnamed x5, waiting for transfers between devices  38.6 us
    all_gather x1, blocking collectives, on_device(): lax.all_gather(d_out, 'col', axis=1, tiled=True)  32.2 us
    all_gather x1, blocking collectives, on_device(): lax.all_gather(queries, 'col', axis=1, tiled=True)  29.7 us
    convert_element_type x2, other arithmetic, on_device(): (weights * (grad_prob - row_delta[..., None])).astype(jnp.bfloat16)  21 us
    convert_element_type x2, local copies, waits for them, and re-layouts, on_device(): (weights * (grad_prob - row_delta[..., None])).astype(jnp.bfloat16)  14.4 us
    dot_general x1, local copies, waits for them, and re-layouts, on_device(): jnp.dot(flat_pair, w_bias, preferred_element_type=jnp.float32)  12.1 us
  transfers between devices with their start and end apart: 4, of which 2 were waited for; matrix products, arithmetic and copies ran while one was open for 18% of the time, Pallas kernels for 0%

commit v1 on v0

--- a/solution.py
+++ b/solution.py
@@ -7,6 +7,11 @@
 H = 96
 P_SIZE = 512
 HD = 16
+
+
+def summed_here(x, mesh_axis):
+    parts = lax.all_gather(x, mesh_axis)
+    return jnp.sum(parts, axis=0)
 
 
 def joined(value, axis, join):
@@ -73,7 +78,7 @@
         .reshape(row_count, col_count, P_SIZE)
     )
     weight_term = jnp.dot(flat_pair.T, score_flat, preferred_element_type=jnp.float32)
-    d_wbias = lax.psum(weight_term, ("row", "col"))
+    d_wbias = summed_here(weight_term, ("row", "col"))
     query_term = (
         jnp.einsum("hij,jhd->ihd", grad_score, key_heads, preferred_element_type=jnp.float32)
         * scale

time: 435 us -> 392 us (0.901)
  waiting for transfers between devices: 101 us -> 48.8 us
  local copies, waits for them, and re-layouts: 48.6 us -> 54.1 us
    psum x1 -> x0, waiting for transfers between devices: 61.9 us -> none  [on_device(): d_wbias = lax.psum(weight_term, ('row', 'col'))]
    unnamed x5, waiting for transfers between devices: 38.6 us -> 48.8 us
    unnamed x18, local copies, waits for them, and re-layouts: 7.11 us -> 12.6 us
  transfers between devices with their start and end apart: 4 -> 4, of which waited for: 2 -> 1; matrix products, arithmetic and copies ran while one was open for 18% -> 20% of each run, Pallas kernels for 0% -> 0%
where the time goes in v1:
time: 392 us; the launch traced here: 389 us
  blocking collectives  170 us (43%)
  matrix products  61.1 us (16%)
  local copies, waits for them, and re-layouts  54.1 us (14%)
  waiting for transfers between devices  48.8 us (12%)
  other arithmetic  39.5 us (10%)
  between operations  15.3 us (4%)
    all_gather x3, blocking collectives, joined(): pieces = jax.tree.map(lambda part: lax.all_gather(part, axis), value)  96.3 us
    unnamed x5, waiting for transfers between devices  48.8 us
    all_gather x1, blocking collectives, on_device(): lax.all_gather(d_out, 'col', axis=1, tiled=True)  32.2 us
    all_gather x1, blocking collectives, on_device(): lax.all_gather(queries, 'col', axis=1, tiled=True)  29.7 us
    convert_element_type x2, other arithmetic, on_device(): (weights * (grad_prob - row_delta[..., None])).astype(jnp.bfloat16)  21 us
    convert_element_type x2, local copies, waits for them, and re-layouts, on_device(): (weights * (grad_prob - row_delta[..., None])).astype(jnp.bfloat16)  14.4 us
    unnamed x18, local copies, waits for them, and re-layouts  12.6 us
    dot_general x1, local copies, waits for them, and re-layouts, on_device(): jnp.dot(flat_pair, w_bias, preferred_element_type=jnp.float32)  12.1 us
  transfers between devices with their start and end apart: 4, of which 1 were waited for; matrix products, arithmetic and copies ran while one was open for 20% of the time, Pallas kernels for 0%

profile of v1, /device:TPU:8, one launch (start us, length us, event | category | flops | bytes accessed | tf_op | source)
XLA Modules:
  0.0 389.4 jit_solution(12814721808830343179)
XLA Ops:
  8.9 11.2 %fusion.11 = f32[192,96,96]{2,1,0:T(8,128)} fusion(bf16[192,96,512]{2,1,0:T(8,128)(2,1)} %param.8, bf16[512,96]{0,1:T(8,128)(2,1)S(1)} %copy-done), kind=kOutput, calls=%fused_computation.28 | convolution fusion | flops 1811939328 | bytes 26050560 | tf_op jit(solution)/shard_map/dot_general | solution.py:52
  20.1 12.1 %copy.40 = f32[192,96,96]{0,1,2:T(8,128)} copy(f32[192,96,96]{2,1,0:T(8,128)} %fusion.11) | data formatting | bytes 14155776 | tf_op jit(solution)/shard_map/dot_general | solution.py:52
  32.4 29.7 %all_gather.36 = bf16[192,1536]{0,1:T(8,128)(2,1)S(1)} all-gather(bf16[192,192]{0,1:T(8,128)(2,1)S(1)} %copy.38), channel_id=1, replica_groups=mesh['row'=4,'col'=8] {'col'}, dimensions={1}, use_global_device_ids=true | all-gather | bytes 663552 | tf_op jit(solution)/shard_map/all_gather | solution.py:40
  62.1 5.9 %all_gather.37 = bf16[96,1536]{1,0:T(8,128)(2,1)S(1)} all-gather(bf16[96,384]{1,0:T(8,128)(2,1)S(1)} %copy-done.5), channel_id=1, replica_groups=mesh['row'=4,'col'=8] {'row'}, dimensions={1}, use_global_device_ids=true | all-gather | bytes 368640 | tf_op jit(solution)/shard_map/all_gather | solution.py:44
  68.4 32.2 %all_gather.42 = bf16[192,1536]{0,1:T(8,128)(2,1)S(1)} all-gather(bf16[192,192]{0,1:T(8,128)(2,1)S(1)} %copy.42), channel_id=1, replica_groups=mesh['row'=4,'col'=8] {'col'}, dimensions={1}, use_global_device_ids=true | all-gather | bytes 663552 | tf_op jit(solution)/shard_map/all_gather | solution.py:41
  100.6 5.9 %all_gather.43 = bf16[96,1536]{1,0:T(8,128)(2,1)S(1)} all-gather(bf16[96,384]{1,0:T(8,128)(2,1)S(1)} %copy-done.6), channel_id=1, replica_groups=mesh['row'=4,'col'=8] {'row'}, dimensions={1}, use_global_device_ids=true | all-gather | bytes 368640 | tf_op jit(solution)/shard_map/all_gather | solution.py:45
  106.7 9.2 %fusion.13 = (f32[96,192]{1,0:T(8,128)S(1)}, f32[96,192,96]{1,2,0:T(8,128)S(1)}, f32[96,192,96]{1,2,0:T(8,128)}) fusion(f32[192,96,96]{0,1,2:T(8,128)} %copy.40, bf16[192,96,16]{0,2,1:T(8,128)(2,1)S(1)} %bitcast.97, bf16[96,96,16]{0,2,1:T(8,128)(2,1)S(1)} %bitcast.102), kind=kOutput, calls=%fused_computation.30 | convolution fusion | flops 61913088 | bytes 22192128 | tf_op jit(solution)/shard_map/ihd,jhd->hij/dot_general | solution.py:56
  115.8 5.7 %multiply_reduce_fusion = (f32[96,192]{1,0:T(8,128)S(1)}, f32[96,192]{1,0:T(8,128)S(1)}, f32[96,192,96]{1,2,0:T(8,128)}) fusion(f32[96,192,96]{1,2,0:T(8,128)S(1)} %get-tuple-element.66, f32[96,192]{1,0:T(8,128)S(1)} %get-tuple-element.65, bf16[192,96,16]{0,2,1:T(8,128)(2,1)S(1)} %bitcast.104, bf16[96,96,16]{0,2,1:T(8,128)(2,1)S(1)} %bitcast.109), kind=kOutput, calls=%fused_computation.19 | convolution fusion | flops 63664128 | bytes 15261696 | tf_op jit(solution)/shard_map/ihd,jhd->hij/dot_general | solution.py:59
  122.1 32.1 %all-gather.1 = f32[768,192]{1,0:T(8,128)S(1)} all-gather(f32[96,192]{1,0:T(8,128)S(1)} %get-tuple-element.48), channel_id=3, replica_groups=mesh['row'=4,'col'=8] {'col'}, dimensions={0}, use_global_device_ids=true | all-gather | bytes 663552 | tf_op jit(solution)/shard_map/all_gather | solution.py:18
  155.2 32.1 %all-gather.2 = f32[768,192]{1,0:T(8,128)S(1)} all-gather(f32[96,192]{1,0:T(8,128)S(1)} %get-tuple-element.47), channel_id=4, replica_groups=mesh['row'=4,'col'=8] {'col'}, dimensions={0}, use_global_device_ids=true | all-gather | bytes 663552 | tf_op jit(solution)/shard_map/all_gather | solution.py:18
  188.2 32.0 %all-gather = f32[768,192]{1,0:T(8,128)S(1)} all-gather(f32[96,192]{1,0:T(8,128)S(1)} %get-tuple-element.65), channel_id=2, replica_groups=mesh['row'=4,'col'=8] {'col'}, dimensions={0}, use_global_device_ids=true | all-gather | bytes 663552 | tf_op jit(solution)/shard_map/all_gather | solution.py:18
  220.3 13.8 %while.14 = (s32[]{:T(128)}, f32[96,192]{1,0:T(8,128)S(1)}, f32[96,192]{1,0:T(8,128)S(1)}, f32[96,192]{1,0:T(8,128)S(1)}, f32[7,96,192]{2,1,0:T(8,128)S(1)}, /*i...) while((s32[]{:T(128)}, f32[96,192]{1,0:T(8,128)S(1)}, f32[96,192]{1,0:T(8,128)S(1)}, ...), condition=%wide.region_4.5_spmd, body=%wide.region_3.4_spmd.sunk | while | flops 202754 | bytes 1032285 | solution.py:21
  234.2 6.2 %fusion.9 = f32[96,96,16]{1,2,0:T(8,128)} fusion(bf16[192,96,16]{0,2,1:T(8,128)(2,1)S(1)} %bitcast.105, f32[96,192,96]{1,2,0:T(8,128)} %copy-done.1, f32[96,192]{1,0:T(8,128)S(1)} %get-tuple-element.45, f32[96,192]{1,0:T(8,128)S(1)} %get-tuple-element.44), kind=kOutput, calls=%fused_computation.23 | convolution fusion | flops 61931520 | bytes 8404992 | tf_op jit(solution)/shard_map/hij,ihd->jhd/dot_general | solution.py:90
  240.3 2.2 copy.51
  242.8 7.9 %multiply_convert_fusion = bf16[96,192,96]{1,2,0:T(8,128)(2,1)S(1)} fusion(f32[96,192,96]{1,2,0:T(8,128)} %get-tuple-element.68, f32[96,192]{1,0:T(8,128)S(1)} %div.21, f32[96,192]{1,0:T(8,128)S(1)} %get-tuple-element.45, f32[96,192,96]{1,2,0:T(8,128)} %copy-done.1, f32[96,192]{1,0:T(8,128)S(1)} %get-tuple-element.44), kind=kLoop, calls=%fused_computation.17 | loop fusion | flops 8847360 | bytes 17915904 | tf_op jit(solution)/shard_map/convert_element_type | solution.py:72
  255.4 4.2 %convolution_multiply_fusion = f32[96,192,16]{1,2,0:T(8,128)} fusion(bf16[96,96,16]{0,2,1:T(8,128)(2,1)S(1)} %bitcast.103, bf16[96,192,96]{1,2,0:T(8,128)(2,1)} %copy-done.2), kind=kOutput, calls=%fused_computation.25 | convolution fusion | flops 56918016 | bytes 5013504 | tf_op jit(solution)/shard_map/hij,jhd->ihd/dot_general | solution.py:83
  259.7 13.1 %fusion.4 = bf16[192,96,96]{0,1,2:T(8,128)(2,1)} fusion(f32[96,192,96]{1,2,0:T(8,128)} %get-tuple-element.68, f32[192,96,96]{0,1,2:T(8,128)} %copy.40, f32[96,192,96]{1,2,0:T(8,128)} %get-tuple-element.67, f32[192,96]{0,1:T(8,128)S(1)} %bitcast.110, f32[192,96]{0,1:T(8,128)S(1)} %bitcast.96, f32[192,96]{0,1:T(8,128)S(1)} %bitcast.95), kind=kLoop, calls=%fused_computation.11 | loop fusion | flops 12386304 | bytes 24993792 | tf_op jit(solution)/shard_map/convert_element_type | solution.py:72
  272.8 7.6 %copy.45 = bf16[192,96,96]{1,2,0:T(8,128)(2,1)} copy(bf16[192,96,96]{0,1,2:T(8,128)(2,1)} %fusion.4) | data formatting | bytes 7077888 | tf_op jit(solution)/shard_map/convert_element_type | solution.py:72
  280.5 11.8 %convolution_bitcast_fusion = f32[512,96]{0,1:T(8,128)} fusion(bf16[192,96,96]{1,2,0:T(8,128)(2,1)} %copy.45, bf16[192,96,512]{2,1,0:T(8,128)(2,1)} %param.8), kind=kOutput, calls=%fused_computation.27 | convolution fusion | flops 1811939328 | bytes 22609920 | tf_op jit(solution)/shard_map/dot_general | solution.py:80
  292.2 6.7 %copy.44 = bf16[192,96,96]{1,0,2:T(8,128)(2,1)} copy(bf16[192,96,96]{0,1,2:T(8,128)(2,1)} %fusion.4) | data formatting | bytes 7077888 | tf_op jit(solution)/shard_map/convert_element_type | solution.py:72
  299.0 9.2 %reshape.49 = bf16[18432,96]{0,1:T(8,128)(2,1)} reshape(bf16[192,96,96]{1,0,2:T(8,128)(2,1)} %copy.44) | data formatting | bytes 7077888 | tf_op jit(solution)/shard_map/reshape | solution.py:74
  308.2 11.5 %convolution_convert_fusion = bf16[18432,512]{1,0:T(8,128)(2,1)} fusion(bf16[18432,96]{0,1:T(8,128)(2,1)} %reshape.49, bf16[512,96]{0,1:T(8,128)(2,1)S(1)} %copy-done), kind=kOutput, calls=%fused_computation.8 | convolution fusion | flops 1821376512 | bytes 22511616 | tf_op jit(solution)/shard_map/dot_general | solution.py:76
  322.9 48.8 %reduce-scatter.10.cloned.1.call-done = f32[192,192]{1,0:T(8,128)} async-done(((f32[1536,192]{1,0:T(8,128)}), f32[192,192]{1,0:T(8,128)}) %reduce-scatter.10.cloned.1.call-update) | async-done | bytes 147472
  373.3 7.1 %copy.57 = f32[12,8,32,512]{3,2,1,0:T(8,128)S(1)} copy(f32[12,8,32,512]{3,1,2,0:T(8,128)} %bitcast.99) | data formatting | bytes 12582912
  (63 shorter events, 29.4 us)
Async XLA Ops:
  8.0 0.9 copy-start
  8.0 311.7 %reduce-scatter.8.cloned.1.call-start = ((), (), s32[]{:S(2)}) async-start(), calls=%async_computation.4 | async-start | bytes 737280 | tf_op jit(solution)/shard_map/reduce_scatter | solution.py:96
  20.1 12.2 %copy-start.3 = (bf16[192,192]{1,0:T(8,128)(2,1)S(1)}, bf16[192,192]{1,0:T(8,128)(2,1)}, u32[]{:S(2)}) copy-start(bf16[192,192]{1,0:T(8,128)(2,1)} %param.10) | copy-start | bytes 221188
  20.1 42.0 %copy-start.5 = (bf16[96,384]{1,0:T(8,128)(2,1)S(1)}, bf16[96,384]{1,0:T(8,128)(2,1)}, u32[]{:S(2)}) copy-start(bf16[96,384]{1,0:T(8,128)(2,1)} %param.11) | copy-start | bytes 221188
  20.1 48.1 %copy-start.4 = (bf16[192,192]{1,0:T(8,128)(2,1)S(1)}, bf16[192,192]{1,0:T(8,128)(2,1)}, u32[]{:S(2)}) copy-start(bf16[192,192]{1,0:T(8,128)(2,1)} %param.13) | copy-start | bytes 221188
  20.1 80.5 %copy-start.6 = (bf16[96,384]{1,0:T(8,128)(2,1)S(1)}, bf16[96,384]{1,0:T(8,128)(2,1)}, u32[]{:S(2)}) copy-start(bf16[96,384]{1,0:T(8,128)(2,1)} %param.12) | copy-start | bytes 221188
  115.8 6.3 %copy-start.1 = (f32[96,192,96]{1,2,0:T(8,128)}, f32[96,192,96]{1,2,0:T(8,128)S(1)}, u32[]{:S(2)}) copy-start(f32[96,192,96]{1,2,0:T(8,128)S(1)} %get-tuple-element.66) | copy-start | bytes 21233668
  242.6 78.7 %reduce-scatter.6.cloned.1.call-start = ((), (), s32[]{:S(2)}) async-start(), calls=%async_computation.3 | async-start | bytes 737280 | tf_op jit(solution)/shard_map/reduce_scatter | solution.py:95
  250.7 2.2 copy-start.2
  255.4 116.3 %reduce-scatter.10.cloned.1.call-start = ((), (), s32[]{:S(2)}) async-start(), calls=%async_computation.6 | async-start | bytes 1769472
  259.7 113.6 %all-gather.6.cloned.1.call-start = ((), (), s32[]{:S(2)}) async-start(), calls=%async_computation.5 | async-start | bytes 6488064 | tf_op jit(solution)/shard_map/all_gather | solution.py:13
Sparse Core Ops, SparseCore 0:
  242.7 25.4 reduce-scatter.7
  270.7 22.0 reduce-scatter.5
  296.2 75.3 reduce-scatter.9
Sparse Core Ops, SparseCore 1:
  292.3 77.8 all-gather.5
